TPU v7x, 32 devices: a whole 2x2x4 slice. The times are simulated.
32 devices in a mesh: row: 8 (over z, core), col: 4 (over y, x).
Axes of the slice: x: 2, y: 2, z: 4, core: 2. Of those that a mesh axis runs over, the one named last changes fastest.
Arguments:
- features: bfloat16 [8192, 256], P(('row', 'col')), may hold values from -6 to 6
- weight_in: bfloat16 [2, 256, 256], replicated, may hold values from -0.21875 to 0.21875
- weight_out: bfloat16 [2, 256, 256], replicated, may hold values from -0.21875 to 0.21875
- weight_self: bfloat16 [2, 256, 256], replicated, may hold values from -0.21875 to 0.21875
- layer_bias: float32 [2, 256], replicated, may hold values from -3 to 3
- out_degree: int32 [8192], P(('row', 'col')), may hold values from 1 to 64
- in_degree: int32 [8192], P(('row', 'col')), may hold values from 1 to 64
- tile_values: bfloat16 [4096, 128, 128], P(('row', 'col')), may hold values from 0 to 1
- tile_pick: int32 [4096], P(('row', 'col')), may hold values from 0 to 3
- tile_count: int32 [32], P(('row', 'col')), may hold values from 1 to 128, as said below
- cotangent: bfloat16 [8192, 256], P(('row', 'col')), may hold values from -6 to 6
Outputs:
- out_features: bfloat16 [8192, 256], P(('row', 'col'))
- grad_features: float32 [8192, 256], P(('row', 'col'))
- grad_weight_in: float32 [2, 256, 256], replicated
- grad_weight_out: float32 [2, 256, 256], replicated
- grad_weight_self: float32 [2, 256, 256], replicated
- grad_bias: float32 [2, 256], replicated
Inputs may be any that keep to these rules, and one draw needn't show every extreme that they name: `tile_count`: slots at or above a device's count are empty and unused; in every draw some device has all 128 slots live. `tile_pick`: slot s of a device belongs to group s // (128 // 32), which fixes the node square of its tile as in the definition of A.
All inputs are finite; a program needn't handle non-finite values.
Results may differ from a plain program's by a relative error of at most 0.025.
Values may be sent and summed in bfloat16 or wider, within the bound.
A program may use at most 128 MiB of HBM per device.

v0:
```python
import jax
import jax.numpy as jnp
from jax import lax
from jax.sharding import PartitionSpec as P


def activation(inputs):
    return jax.nn.gelu(inputs, approximate=True)


def dense_block(tile_values, tile_pick, tile_count, row_count, col_count, sub_blocks):
    tile_total, tile_size, unused = tile_values.shape
    per_peer = tile_total // (row_count * col_count)
    live = jnp.arange(tile_total, dtype=jnp.int32) < tile_count[0]
    picks = jnp.where(live, tile_pick, -1).reshape(row_count * col_count, per_peer)
    tiles = tile_values.reshape(row_count * col_count, per_peer, tile_size, tile_size)
    rows = []
    for row_half in range(sub_blocks):
        cols = []
        for col_half in range(sub_blocks):
            spot = row_half * sub_blocks + col_half
            total = 0.0
            for slot in range(per_peer):
                total = total + jnp.where(
                    (picks[:, slot] == spot)[:, None, None], tiles[:, slot].astype(jnp.float32), 0.0
                )
            cols.append(total.astype(jnp.bfloat16))
        rows.append(jnp.concatenate(cols, axis=2))
    squares = jnp.concatenate(rows, axis=1)
    side = sub_blocks * tile_size
    squares = squares.reshape(row_count, col_count, side, side)
    return squares.transpose(1, 2, 0, 3).reshape(col_count * side, row_count * side)


def per_device(
    features,
    weight_in,
    weight_out,
    weight_self,
    layer_bias,
    out_degree,
    in_degree,
    tile_values,
    tile_pick,
    tile_count,
    cotangent,
):
    row_count = lax.axis_size("row")
    col_count = lax.axis_size("col")
    sub_blocks = features.shape[0] // tile_values.shape[1]
    block = dense_block(tile_values, tile_pick, tile_count, row_count, col_count, sub_blocks)
    scale_in = 1.0 / jnp.sqrt(in_degree.astype(jnp.float32))
    scale_out = 1.0 / jnp.sqrt(out_degree.astype(jnp.float32))

    def forward_messages(first, second):
        row_rows = lax.all_gather(second, "col", axis=0, tiled=True)
        column_rows = lax.all_gather(first, "row", axis=0, tiled=True)
        reverse = lax.dot_general(
            block, row_rows, (((0,), (0,)), ((), ())), preferred_element_type=jnp.float32
        )
        direct = jnp.dot(block, column_rows, preferred_element_type=jnp.float32)
        summed_reverse = lax.psum_scatter(reverse, "row", scatter_dimension=0, tiled=True)
        pieces = direct.astype(jnp.bfloat16).reshape((lax.axis_size("col"), -1, direct.shape[1]))
        pieces = lax.all_to_all(pieces, "col", 0, 0, tiled=True)
        summed_direct = jnp.sum(pieces.astype(jnp.float32), axis=0)
        return (summed_direct, summed_reverse)

    layer_total = weight_in.shape[0]
    hidden = features
    stored = []
    for layer in range(layer_total):
        hidden_wide = hidden.astype(jnp.float32)
        scaled_in = (scale_in[:, None] * hidden_wide).astype(jnp.bfloat16)
        scaled_out = (scale_out[:, None] * hidden_wide).astype(jnp.bfloat16)
        summed_direct, summed_reverse = forward_messages(scaled_in, scaled_out)
        msg_in = (scale_out[:, None] * summed_direct).astype(jnp.bfloat16)
        msg_out = (scale_in[:, None] * summed_reverse).astype(jnp.bfloat16)
        preact = jnp.dot(msg_in, weight_in[layer], preferred_element_type=jnp.float32)
        preact = preact + jnp.dot(msg_out, weight_out[layer], preferred_element_type=jnp.float32)
        preact = preact + jnp.dot(hidden, weight_self[layer], preferred_element_type=jnp.float32)
        preact = preact + layer_bias[layer][None, :]
        stored.append((hidden, msg_in, msg_out, preact))
        hidden = activation(preact).astype(jnp.bfloat16)
    out_features = hidden
    upstream = cotangent.astype(jnp.float32)
    ones = jnp.ones((features.shape[0], 256), jnp.bfloat16)
    grads = []
    for layer in reversed(range(layer_total)):
        hidden, msg_in, msg_out, preact = stored[layer]
        unused, pullback = jax.vjp(activation, preact)
        grad_z = pullback(upstream)[0].astype(jnp.bfloat16)
        parts = jnp.concatenate([msg_in, msg_out, hidden, ones], axis=1)
        grads.append(jnp.einsum("nf,ng->fg", parts, grad_z, preferred_element_type=jnp.float32))
        back_in = (
            scale_out[:, None]
            * jnp.dot(grad_z, weight_in[layer].T, preferred_element_type=jnp.float32)
        ).astype(jnp.bfloat16)
        back_out = (
            scale_in[:, None]
            * jnp.dot(grad_z, weight_out[layer].T, preferred_element_type=jnp.float32)
        ).astype(jnp.bfloat16)
        backward_summed_direct, backward_summed_reverse = forward_messages(back_out, back_in)
        upstream = (
            scale_out[:, None] * backward_summed_direct
            + scale_in[:, None] * backward_summed_reverse
        )
        upstream = upstream + jnp.dot(
            grad_z, weight_self[layer].T, preferred_element_type=jnp.float32
        )
    width = features.shape[1]
    total = jnp.concatenate(grads[::-1], axis=0)
    total = lax.psum_scatter(total, "row", scatter_dimension=0, tiled=True)
    total = lax.psum_scatter(total, "col", scatter_dimension=0, tiled=True)
    total = lax.all_gather(total, ("row", "col"), axis=0, tiled=True)
    total = total.reshape(layer_total, -1, width)
    return (
        out_features,
        upstream,
        total[:, :width],
        total[:, width : 2 * width],
        total[:, 2 * width : 3 * width],
        total[:, 3 * width],
    )


def solution(mesh):
    return jax.shard_map(
        per_device,
        mesh=mesh,
        in_specs=(
            P(("row", "col"), None),
            P(),
            P(),
            P(),
            P(),
            P(("row", "col")),
            P(("row", "col")),
            P(("row", "col"), None, None),
            P(("row", "col")),
            P(("row", "col")),
            P(("row", "col"), None),
        ),
        out_specs=(P(("row", "col"), None), P(("row", "col"), None), P(), P(), P(), P()),
        check_vma=False,
    )
```

profile of v0, /device:TPU:0, one launch (start us, length us, event | category | flops | bytes accessed | tf_op | source)
XLA Modules:
  0.0 429.6 jit_solution(17725921120352170777)
XLA Ops:
  7.2 1.0 copy.100
  8.2 0.7 convert_rsqrt_fusion
  11.5 3.9 fusion.3
  15.5 2.3 fusion.7
  18.5 2.4 copy.99
  20.9 1.5 copy.140
  22.4 15.1 %all_gather.28 = bf16[1024,256]{0,1:T(8,128)(2,1)S(1)} all-gather(bf16[256,256]{0,1:T(8,128)(2,1)S(1)} %get-tuple-element.63), channel_id=1, replica_groups=mesh['row'=8,'col'=4] {'col'}, dimensions={0}, use_global_device_ids=true | all-gather | bytes 655360 | tf_op jit(solution)/shard_map/all_gather | solution.py:56
  37.5 2.6 fusion.89
  40.2 4.6 %convolution_convert_fusion.3 = bf16[1024,256]{1,0:T(8,128)(2,1)} fusion(bf16[1024,2048]{1,0:T(8,128)(2,1)} %bitcast.138, bf16[2048,256]{0,1:T(8,128)(2,1)} %all-gather.6.cloned.1.call-done), kind=kOutput, calls=%fused_computation.37 | convolution fusion | flops 1074003968 | bytes 5767168 | tf_op jit(solution)/shard_map/dot_general | solution.py:61
  44.7 3.6 all-to-all-start
  48.4 6.9 %all-to-all-done = bf16[4,256,256]{2,1,0:T(8,128)(2,1)S(1)} async-done(((bf16[4,256,256]{2,1,0:T(8,128)(2,1)}), bf16[4,256,256]{2,1,0:T(8,128)(2,1)S(1)}, u32[]{:S(2)}, u32[]{:S(2)}) %all-to-all-start) | async-done | bytes 524320 | tf_op jit(solution)/shard_map/all_to_all | solution.py:64
  55.8 20.6 %reduce-scatter.7.cloned.1.call-done = f32[256,256]{0,1:T(8,128)} async-done(((f32[2048,256]{0,1:T(8,128)}), f32[256,256]{0,1:T(8,128)}) %reduce-scatter.7.cloned.1.call-update) | async-done | bytes 262160 | tf_op jit(solution)/shard_map/reduce_scatter | solution.py:62
  76.4 1.0 multiply_convert_fusion.4
  77.7 1.0 fusion.39
  78.7 12.2 %all_gather.30 = bf16[1024,256]{0,1:T(8,128)(2,1)S(1)} all-gather(bf16[256,256]{0,1:T(8,128)(2,1)S(1)} %get-tuple-element.52), channel_id=1, replica_groups=mesh['row'=8,'col'=4] {'col'}, dimensions={0}, use_global_device_ids=true | all-gather | bytes 655360 | tf_op jit(solution)/shard_map/all_gather | solution.py:56
  90.9 4.8 %fusion.90 = f32[2048,256]{0,1:T(8,128)} fusion(bf16[1024,256]{0,1:T(8,128)(2,1)S(1)} %all_gather.30, bf16[1024,2048]{1,0:T(8,128)(2,1)} %bitcast.139), kind=kOutput, calls=%fused_computation.166 | convolution fusion | flops 1073741824 | bytes 6815744 | tf_op jit(solution)/shard_map/dot_general | solution.py:58
  95.9 35.4 %reduce-scatter.9.cloned.1.call-done = f32[256,256]{0,1:T(8,128)} async-done(((f32[2048,256]{0,1:T(8,128)}), f32[256,256]{0,1:T(8,128)}) %reduce-scatter.9.cloned.1.call-update) | async-done | bytes 262160 | tf_op jit(solution)/shard_map/reduce_scatter | solution.py:62
  131.4 1.7 multiply_convert_fusion.1
  133.1 22.9 %all-gather.8.cloned.1.call-done = bf16[2048,256]{0,1:T(8,128)(2,1)} async-done(((bf16[256,256]{0,1:T(8,128)(2,1)}), bf16[2048,256]{0,1:T(8,128)(2,1)}) %all-gather.8.cloned.1.call-update) | async-done | bytes 1048592 | tf_op jit(solution)/shard_map/all_gather | solution.py:57
  156.0 4.6 %convolution_convert_fusion.2 = bf16[1024,256]{1,0:T(8,128)(2,1)} fusion(bf16[1024,2048]{1,0:T(8,128)(2,1)} %bitcast.140, bf16[2048,256]{0,1:T(8,128)(2,1)} %all-gather.8.cloned.1.call-done), kind=kOutput, calls=%fused_computation.36 | convolution fusion | flops 1074003968 | bytes 5767168 | tf_op jit(solution)/shard_map/dot_general | solution.py:61
  160.6 3.5 all-to-all-start.1
  164.2 8.5 %all-to-all-done.1 = bf16[4,256,256]{2,1,0:T(8,128)(2,1)S(1)} async-done(((bf16[4,256,256]{2,1,0:T(8,128)(2,1)}), bf16[4,256,256]{2,1,0:T(8,128)(2,1)S(1)}, u32[]{:S(2)}, u32[]{:S(2)}) %all-to-all-start.1) | async-done | bytes 524320 | tf_op jit(solution)/shard_map/all_to_all | solution.py:64
  173.8 0.8 fusion.18
  175.0 12.4 %all_gather.32 = bf16[1024,256]{0,1:T(8,128)(2,1)S(1)} all-gather(bf16[256,256]{0,1:T(8,128)(2,1)S(1)} %fusion.19), channel_id=1, replica_groups=mesh['row'=8,'col'=4] {'col'}, dimensions={0}, use_global_device_ids=true | all-gather | bytes 655360 | tf_op jit(solution)/shard_map/all_gather | solution.py:56
  187.4 4.8 %fusion.91 = f32[2048,256]{0,1:T(8,128)} fusion(bf16[1024,256]{0,1:T(8,128)(2,1)S(1)} %all_gather.32, bf16[1024,2048]{1,0:T(8,128)(2,1)} %bitcast.141), kind=kOutput, calls=%fused_computation.167 | convolution fusion | flops 1073741824 | bytes 6815744 | tf_op jit(solution)/shard_map/dot_general | solution.py:58
  192.3 5.5 %all-gather.10.cloned.1.call-done = bf16[2048,256]{0,1:T(8,128)(2,1)} async-done(((bf16[256,256]{0,1:T(8,128)(2,1)}), bf16[2048,256]{0,1:T(8,128)(2,1)}) %all-gather.10.cloned.1.call-update) | async-done | bytes 1048592 | tf_op jit(solution)/shard_map/all_gather | solution.py:57
  197.8 4.6 %convolution_convert_fusion.1 = bf16[1024,256]{1,0:T(8,128)(2,1)} fusion(bf16[1024,2048]{1,0:T(8,128)(2,1)} %bitcast.142, bf16[2048,256]{0,1:T(8,128)(2,1)} %all-gather.10.cloned.1.call-done), kind=kOutput, calls=%fused_computation.35 | convolution fusion | flops 1074003968 | bytes 5767168 | tf_op jit(solution)/shard_map/dot_general | solution.py:61
  202.4 3.5 all-to-all-start.2
  206.3 8.2 %all-to-all-done.2 = bf16[4,256,256]{2,1,0:T(8,128)(2,1)S(1)} async-done(((bf16[4,256,256]{2,1,0:T(8,128)(2,1)}), bf16[4,256,256]{2,1,0:T(8,128)(2,1)S(1)}, u32[]{:S(2)}, u32[]{:S(2)}) %all-to-all-start.2) | async-done | bytes 524320 | tf_op jit(solution)/shard_map/all_to_all | solution.py:64
  214.7 20.1 %reduce-scatter.11.cloned.1.call-done = f32[256,256]{0,1:T(8,128)} async-done(((f32[2048,256]{0,1:T(8,128)}), f32[256,256]{0,1:T(8,128)}) %reduce-scatter.11.cloned.1.call-update) | async-done | bytes 262160 | tf_op jit(solution)/shard_map/reduce_scatter | solution.py:62
  234.8 1.3 fusion.51
  236.5 1.5 pad_maximum_fusion
  238.1 34.5 %reduce-scatter.15.cloned.1.call-done = f32[256,256]{1,0:T(8,128)} async-done(((f32[2048,256]{1,0:T(8,128)}), f32[256,256]{1,0:T(8,128)}) %reduce-scatter.15.cloned.1.call-update) | async-done | bytes 262160 | tf_op jit(solution)/shard_map/reduce_scatter | solution.py:112
  272.6 0.8 fusion.20
  273.8 12.7 %all_gather.34 = bf16[1024,256]{0,1:T(8,128)(2,1)S(1)} all-gather(bf16[256,256]{0,1:T(8,128)(2,1)S(1)} %fusion.21), channel_id=1, replica_groups=mesh['row'=8,'col'=4] {'col'}, dimensions={0}, use_global_device_ids=true | all-gather | bytes 655360 | tf_op jit(solution)/shard_map/all_gather | solution.py:56
  286.4 4.8 %fusion.92 = f32[2048,256]{0,1:T(8,128)} fusion(bf16[1024,256]{0,1:T(8,128)(2,1)S(1)} %all_gather.34, bf16[1024,2048]{1,0:T(8,128)(2,1)} %bitcast.143), kind=kOutput, calls=%fused_computation.168 | convolution fusion | flops 1073741824 | bytes 6815744 | tf_op jit(solution)/shard_map/dot_general | solution.py:58
  291.3 7.0 %reduce-scatter.17.cloned.1.call-done = f32[64,256]{1,0:T(8,128)} async-done(((f32[256,256]{1,0:T(8,128)}), f32[64,256]{1,0:T(8,128)}) %reduce-scatter.17.cloned.1.call-update) | async-done | bytes 65552 | tf_op jit(solution)/shard_map/reduce_scatter | solution.py:113
  298.4 26.1 %all-gather.12.cloned.1.call-done = bf16[2048,256]{0,1:T(8,128)(2,1)} async-done(((bf16[256,256]{0,1:T(8,128)(2,1)}), bf16[2048,256]{0,1:T(8,128)(2,1)}) %all-gather.12.cloned.1.call-update) | async-done | bytes 1048592 | tf_op jit(solution)/shard_map/all_gather | solution.py:57
  324.4 4.6 %convolution_convert_fusion = bf16[1024,256]{1,0:T(8,128)(2,1)} fusion(bf16[1024,2048]{1,0:T(8,128)(2,1)} %bitcast.144, bf16[2048,256]{0,1:T(8,128)(2,1)} %all-gather.12.cloned.1.call-done), kind=kOutput, calls=%fused_computation.34 | convolution fusion | flops 1074003968 | bytes 5767168 | tf_op jit(solution)/shard_map/dot_general | solution.py:61
  329.0 3.5 all-to-all-start.3
  332.5 0.8 copy.121
  333.2 7.9 %all-to-all-done.3 = bf16[4,256,256]{2,1,0:T(8,128)(2,1)S(1)} async-done(((bf16[4,256,256]{2,1,0:T(8,128)(2,1)}), bf16[4,256,256]{2,1,0:T(8,128)(2,1)S(1)}, u32[]{:S(2)}, u32[]{:S(2)}) %all-to-all-start.3) | async-done | bytes 524320 | tf_op jit(solution)/shard_map/all_to_all | solution.py:64
  341.4 20.1 %reduce-scatter.13.cloned.1.call-done = f32[256,256]{0,1:T(8,128)} async-done(((f32[2048,256]{0,1:T(8,128)}), f32[256,256]{0,1:T(8,128)}) %reduce-scatter.13.cloned.1.call-update) | async-done | bytes 262160 | tf_op jit(solution)/shard_map/reduce_scatter | solution.py:62
  361.4 1.1 convolution_add_fusion
  362.6 0.8 copy.122
  363.4 55.8 %all-gather.14.cloned.1.call-done = f32[2048,256]{1,0:T(8,128)} async-done(((f32[64,256]{1,0:T(8,128)}), f32[2048,256]{1,0:T(8,128)}) %all-gather.14.cloned.1.call-update) | async-done | bytes 2097168 | tf_op jit(solution)/shard_map/all_gather | solution.py:114
  419.2 2.5 fusion.87
  421.7 0.7 slice.121
  (68 shorter events, 7.3 us)
Async XLA Ops:
  7.2 33.0 %all-gather.6.cloned.1.call-start = ((), (), s32[]{:S(2)}) async-start(), calls=%async_computation.10 | async-start | bytes 1179648 | tf_op jit(solution)/shard_map/all_gather | solution.py:57
  9.7 66.8 %reduce-scatter.7.cloned.1.call-start = ((), (), s32[]{:S(2)}) async-start(), calls=%async_computation.11 | async-start | bytes 2359296 | tf_op jit(solution)/shard_map/reduce_scatter | solution.py:62
  11.5 4.0 copy-start
  22.4 15.1 %copy-start.1 = (bf16[128,8,8,256]{3,1,2,0:T(8,128)(2,1)}, bf16[128,8,8,256]{3,1,2,0:T(8,128)(2,1)S(1)}, u32[]{:S(2)}) copy-start(bf16[128,8,8,256]{3,1,2,0:T(8,128)(2,1)S(1)} %copy.140) | copy-start | bytes 12582916
  40.1 8.3 %copy-start.7 = (f32[2,256]{1,0:T(2,128)S(1)}, f32[2,256]{1,0:T(2,128)}, u32[]{:S(2)}) copy-start(f32[2,256]{1,0:T(2,128)} %param.15) | copy-start | bytes 6148
  44.7 10.8 %copy-start.3 = (bf16[2,256,256]{2,1,0:T(8,128)(2,1)S(1)}, bf16[2,256,256]{2,1,0:T(8,128)(2,1)}, u32[]{:S(2)}) copy-start(bf16[2,256,256]{2,1,0:T(8,128)(2,1)} %param.12) | copy-start | bytes 786436
  44.7 32.7 %copy-start.2 = (bf16[2,256,256]{2,1,0:T(8,128)(2,1)S(1)}, bf16[2,256,256]{2,1,0:T(8,128)(2,1)}, u32[]{:S(2)}) copy-start(bf16[2,256,256]{2,1,0:T(8,128)(2,1)} %param.13) | copy-start | bytes 786436
  44.7 32.9 %copy-start.4 = (bf16[256,256]{1,0:T(8,128)(2,1)S(1)}, bf16[256,256]{1,0:T(8,128)(2,1)}, u32[]{:S(2)}) copy-start(bf16[256,256]{1,0:T(8,128)(2,1)} %param.11) | copy-start | bytes 393220
  44.7 32.9 %copy-start.6 = (bf16[2,256,256]{2,1,0:T(8,128)(2,1)S(1)}, bf16[2,256,256]{2,1,0:T(8,128)(2,1)}, u32[]{:S(2)}) copy-start(bf16[2,256,256]{2,1,0:T(8,128)(2,1)} %param.14) | copy-start | bytes 786436
  44.7 10.6 %all-to-all-start = ((bf16[4,256,256]{2,1,0:T(8,128)(2,1)}), bf16[4,256,256]{2,1,0:T(8,128)(2,1)S(1)}, u32[]{:S(2)}, u32[]{:S(2)}) async-start(bf16[4,256,256]{2,1,0:T(8,128)(2,1)} %bitcast.12), calls=%async_computation | async-start | bytes 1048576 | tf_op jit(solution)/shard_map/all_to_all | solution.py:64
  48.4 83.0 %reduce-scatter.9.cloned.1.call-start = ((), (), s32[]{:S(2)}) async-start(), calls=%async_computation.13 | async-start | bytes 2359296 | tf_op jit(solution)/shard_map/reduce_scatter | solution.py:62
  95.7 60.3 %all-gather.8.cloned.1.call-start = ((), (), s32[]{:S(2)}) async-start(), calls=%async_computation.12 | async-start | bytes 1179648 | tf_op jit(solution)/shard_map/all_gather | solution.py:57
  133.1 31.0 %copy-start.5 = (bf16[256,256]{1,0:T(8,128)(2,1)S(1)}, bf16[256,256]{1,0:T(8,128)(2,1)}, u32[]{:S(2)}) copy-start(bf16[256,256]{1,0:T(8,128)(2,1)} %param.21) | copy-start | bytes 393220
  160.6 12.1 %all-to-all-start.1 = ((bf16[4,256,256]{2,1,0:T(8,128)(2,1)}), bf16[4,256,256]{2,1,0:T(8,128)(2,1)S(1)}, u32[]{:S(2)}, u32[]{:S(2)}) async-start(bf16[4,256,256]{2,1,0:T(8,128)(2,1)} %bitcast.17), calls=%async_computation.2 | async-start | bytes 1048576 | tf_op jit(solution)/shard_map/all_to_all | solution.py:64
  164.0 33.8 %all-gather.10.cloned.1.call-start = ((), (), s32[]{:S(2)}) async-start(), calls=%async_computation.14 | async-start | bytes 1179648 | tf_op jit(solution)/shard_map/all_gather | solution.py:57
  174.7 60.1 %reduce-scatter.11.cloned.1.call-start = ((), (), s32[]{:S(2)}) async-start(), calls=%async_computation.15 | async-start | bytes 2359296 | tf_op jit(solution)/shard_map/reduce_scatter | solution.py:62
  202.4 12.1 %all-to-all-start.2 = ((bf16[4,256,256]{2,1,0:T(8,128)(2,1)}), bf16[4,256,256]{2,1,0:T(8,128)(2,1)S(1)}, u32[]{:S(2)}, u32[]{:S(2)}) async-start(bf16[4,256,256]{2,1,0:T(8,128)(2,1)} %bitcast.22), calls=%async_computation.4 | async-start | bytes 1048576 | tf_op jit(solution)/shard_map/all_to_all | solution.py:64
  205.9 66.7 %reduce-scatter.15.cloned.1.call-start = ((), (), s32[]{:S(2)}) async-start(), calls=%async_computation.18 | async-start | bytes 2359296 | tf_op jit(solution)/shard_map/reduce_scatter | solution.py:112
  238.0 60.3 %reduce-scatter.17.cloned.1.call-start = ((), (), s32[]{:S(2)}) async-start(), calls=%async_computation.19 | async-start | bytes 327680 | tf_op jit(solution)/shard_map/reduce_scatter | solution.py:113
  272.6 51.8 %all-gather.12.cloned.1.call-start = ((), (), s32[]{:S(2)}) async-start(), calls=%async_computation.16 | async-start | bytes 1179648 | tf_op jit(solution)/shard_map/all_gather | solution.py:57
  273.5 87.9 %reduce-scatter.13.cloned.1.call-start = ((), (), s32[]{:S(2)}) async-start(), calls=%async_computation.17 | async-start | bytes 2359296 | tf_op jit(solution)/shard_map/reduce_scatter | solution.py:62
  291.3 128.0 %all-gather.14.cloned.1.call-start = ((), (), s32[]{:S(2)}) async-start(), calls=%async_computation.20 | async-start | bytes 2162688 | tf_op jit(solution)/shard_map/all_gather | solution.py:114
  329.0 12.2 %all-to-all-start.3 = ((bf16[4,256,256]{2,1,0:T(8,128)(2,1)}), bf16[4,256,256]{2,1,0:T(8,128)(2,1)S(1)}, u32[]{:S(2)}, u32[]{:S(2)}) async-start(bf16[4,256,256]{2,1,0:T(8,128)(2,1)} %bitcast.23), calls=%async_computation.6 | async-start | bytes 1048576 | tf_op jit(solution)/shard_map/all_to_all | solution.py:64
Sparse Core Ops, SparseCore 0:
  10.1 26.6 all-gather.5
  40.2 36.1 reduce-scatter.6
  95.8 35.5 reduce-scatter.8
  133.4 22.5 all-gather.7
  174.8 22.9 all-gather.9
  199.9 34.8 reduce-scatter.10
  238.1 34.3 reduce-scatter.14
  275.3 22.9 reduce-scatter.16
  300.5 23.8 all-gather.11
  326.6 34.8 reduce-scatter.12
  364.3 54.8 all-gather.13
where the time goes:
time: 430 us
  waiting for transfers between devices  280 us (65%)
  blocking collectives  52.4 us (12%)
  matrix products  42.9 us (10%)
  between operations  14.9 us (3%)
  starting transfers between devices  14.7 us (3%)
  other arithmetic  13.8 us (3%)
  local copies, waits for them, and re-layouts  11.1 us (3%)
    reduce_scatter x4, waiting for transfers between devices, forward_messages(): lax.psum_scatter(reverse, 'row', scatter_dimension=0, tiled=True)  96.2 us
    all_gather x1, waiting for transfers between devices, per_device(): total = lax.all_gather(total, ('row', 'col'), axis=0, tiled=True)  55.8 us
    all_gather x4, waiting for transfers between devices, forward_messages(): column_rows = lax.all_gather(first, 'row', axis=0, tiled=True)  54.6 us
    all_gather x4, blocking collectives, forward_messages(): row_rows = lax.all_gather(second, 'col', axis=0, tiled=True)  52.4 us
    reduce_scatter x1, waiting for transfers between devices, per_device(): total = lax.psum_scatter(total, 'row', scatter_dimension=0, tiled=True)  34.5 us
    all_to_all x4, waiting for transfers between devices, forward_messages(): pieces = lax.all_to_all(pieces, 'col', 0, 0, tiled=True)  31.5 us
    dot_general x4, matrix products, forward_messages(): direct = jnp.dot(block, column_rows, preferred_element_type=jnp.float32)  18.3 us
    dot_general x4, matrix products, forward_messages(): lax.dot_general(block, row_rows, (((0,), (0,)), ((), ())), preferred_elem...  17.1 us
  transfers between devices with their start and end apart: 15, of which 14 were waited for; matrix products, arithmetic and copies ran while one was open for 10% of the time, Pallas kernels for 0%

commit v1 on v0

v1 whole, which is shorter than its diff:
```python
import functools

import jax
import jax.numpy as jnp
from jax import lax
from jax.experimental import pallas as pl
from jax.experimental.pallas import tpu as pltpu
from jax.sharding import PartitionSpec as P

MESH = pl.DeviceIdType.MESH
F32 = jnp.float32
BF16 = jnp.bfloat16
EXTRA = 16
C0 = 0.7978845608028654
C1 = 0.044715


def gelu(v):
    return 0.5 * v * (1.0 + jnp.tanh(C0 * (v + C1 * (v * v * v))))


def gelu_slope(v):
    t = jnp.tanh(C0 * (v + C1 * (v * v * v)))
    return 0.5 * (1.0 + t) + 0.5 * v * (1.0 - t * t) * (C0 * (1.0 + 3.0 * C1 * (v * v)))


def dot(a, b):
    return jnp.dot(a, b, preferred_element_type=F32)


def dot_nt(a, b):
    return lax.dot_general(a, b, (((1,), (1,)), ((), ())), preferred_element_type=F32)


def dot_tn(a, b):
    return lax.dot_general(a, b, (((0,), (0,)), ((), ())), preferred_element_type=F32)


def kernel(
    rows,
    cols,
    feat,
    w_in,
    w_out,
    w_self,
    bias,
    out_deg,
    in_deg,
    cot,
    pick,
    count,
    tiles,
    out_ref,
    gfeat_ref,
    parts_ref,
    block,
    sib_block,
    staged,
    xc,
    xr,
    send_d,
    recv_d,
    send_r,
    recv_r,
    own_d,
    own_r,
    s_in,
    s_out,
    hs,
    ms_in,
    ms_out,
    zs,
    up,
    gz_ref,
    tile_sem,
    blk_sem,
    xr_sem,
    xrs_sem,
    xcr_sem,
    xcl_sem,
    xcs_sem,
    d_sem,
    r_sem,
):
    chips = rows // 2
    nodes, width = feat.shape
    layers = w_in.shape[0]
    tile = staged.shape[1]
    sub = nodes // tile
    slots = staged.shape[0]
    per = slots // (rows * cols)
    row = lax.axis_index("row")
    c = lax.axis_index("col")
    k = lax.rem(row, 2)
    z = row // 2
    other = 1 - k
    sibling = (2 * z + other, c)

    def remote(src, dst, sems, index, device, parity=None):
        where = (index,) if parity is None else (parity, index)
        return pltpu.make_async_remote_copy(
            src_ref=src,
            dst_ref=dst,
            send_sem=sems.at[(0,) + where],
            recv_sem=sems.at[(1,) + where],
            device_id=device,
            device_id_type=MESH,
        )

    def at_chip(zz):
        return (2 * zz + k, c)

    def at_col(cc):
        return (row, cc)

    barrier = pltpu.get_barrier_semaphore()
    pl.semaphore_signal(barrier, inc=1, device_id=sibling, device_id_type=MESH)
    for off in range(1, chips):
        pl.semaphore_signal(
            barrier, inc=1, device_id=at_chip(lax.rem(z + off, chips)), device_id_type=MESH
        )
    for off in range(1, cols):
        pl.semaphore_signal(
            barrier, inc=1, device_id=at_col(lax.rem(c + off, cols)), device_id_type=MESH
        )

    strip = cols * per

    def tile_copy(rr):
        span = pl.ds(rr * strip, strip)
        return pltpu.make_async_copy(tiles.at[span], staged.at[span], tile_sem.at[rr])

    for kk in (other, k):
        for zz in range(chips):
            tile_copy(2 * zz + kk).start()

    for deg, scale in ((out_deg, s_out), (in_deg, s_in)):
        line = 1.0 / jnp.sqrt(deg[...].astype(F32))
        scale[...] = jnp.transpose(jnp.broadcast_to(line, (width, nodes)))
    hs[0] = feat[...]

    pl.semaphore_wait(barrier, chips + cols - 1)

    def build():
        for kk in (other, k):

            @pl.loop(0, chips)
            def _(zz):
                rr = 2 * zz + kk
                tile_copy(rr).wait()

                @pl.loop(0, cols)
                def _(cc):
                    first = (rr * cols + cc) * per
                    values = []
                    weights = []
                    for s in range(per):
                        values.append(staged[first + s].astype(F32))
                        live = first + s < count[0]
                        weights.append(jnp.where(live, pick[first + s], -1))
                    for spot in range(sub * sub):
                        total = jnp.zeros((tile, tile), F32)
                        for s in range(per):
                            factor = jnp.where(weights[s] == spot, 1.0, 0.0)
                            total = total + factor * values[s]
                        top = pl.multiple_of(cc * nodes + (spot // sub) * tile, tile)
                        left = pl.multiple_of(zz * nodes + (spot % sub) * tile, tile)
                        block[kk, pl.ds(top, tile), pl.ds(left, tile)] = total.astype(BF16)

            if kk is other:
                remote(block.at[other], sib_block, blk_sem, 0, sibling).start()

    def window(zz):
        return pl.ds(pl.multiple_of(zz * nodes, nodes), nodes)

    def exchange(stage, first, second_t):
        p = lax.rem(stage, 2)

        def xr_copy(off):
            mine = xr.at[p, k, :, window(c)]
            return remote(mine, mine, xr_sem, off, at_col(lax.rem(c + off, cols)), p)

        def xrs_copy(off, kk):
            view = xr.at[p, kk, :, window(lax.rem(c + cols - off, cols))]
            return remote(view, view, xrs_sem, off, sibling, p)

        def xc_view(kk, zz):
            return xc.at[p, kk, window(zz), :]

        def xcr_copy(dist, zz):
            return remote(xc_view(k, zz), xc_view(k, zz), xcr_sem, dist, at_chip(z + 1), p)

        def xcl_copy(dist, zz):
            return remote(xc_view(k, zz), xc_view(k, zz), xcl_sem, dist, at_chip(z - 1), p)

        def xcs_copy(kk, zz):
            return remote(xc_view(kk, zz), xc_view(kk, zz), xcs_sem, zz, sibling, p)

        def d_copy(off):
            target = at_col(lax.rem(c + off, cols))
            return remote(send_d.at[off], recv_d.at[p, off], d_sem, off, target, p)

        def r_copy(off):
            target = at_chip(lax.rem(z + off, chips))
            return remote(send_r.at[off], recv_r.at[p, off], r_sem, off, target, p)

        xr[p, k, :, window(c)] = second_t
        xc[p, k, window(z), :] = first
        for off in range(1, cols):
            xr_copy(off).start()
        xrs_copy(0, k).start()

        @pl.when(z + 1 < chips)
        def _():
            xcr_copy(1, z).start()

        @pl.when(z > 0)
        def _():
            xcl_copy(1, z).start()

        xcs_copy(k, z).start()

        @pl.when(stage == 0)
        def _():
            build()

        def take_xr(off):
            source = lax.rem(c + cols - off, cols)
            view = xr.at[p, k, :, window(source)]
            remote(view, view, xr_sem, off, at_col(source), p).wait_recv()
            xrs_copy(off, k).start()

        def take_xc(dist):
            @pl.when(z - dist >= 0)
            def _():
                xcr_copy(dist, z - dist).wait_recv()

                @pl.when(z + 1 < chips)
                def _():
                    xcr_copy(dist + 1, z - dist).start()

                xcs_copy(k, z - dist).start()

            @pl.when(z + dist < chips)
            def _():
                xcl_copy(dist, z + dist).wait_recv()

                @pl.when(z > 0)
                def _():
                    xcl_copy(dist + 1, z + dist).start()

                xcs_copy(k, z + dist).start()

        for off in range(1, cols):
            take_xr(off)
            if off == 1:
                take_xc(1)
        for off in range(cols):
            xrs_copy(off, other).wait_recv()

        @pl.when(stage == 0)
        def _():
            remote(block.at[other], sib_block, blk_sem, 0, sibling).wait_recv()

        lanes = lax.broadcasted_iota(jnp.int32, (EXTRA, nodes), 1)
        groups = lax.broadcasted_iota(jnp.int32, (EXTRA, nodes), 0) // (EXTRA // sub)
        chooser = jnp.where(lanes == groups * tile, 1.0, 0.0).astype(BF16)

        @pl.loop(0, chips)
        def _(step):
            off = lax.rem(step + 1, chips)
            at = window(lax.rem(z + off, chips))
            piece = dot(xr[p, k], block[k, :, at]) + dot(xr[p, other], sib_block[:, at])

            @pl.when(off > 0)
            def _():
                means = []
                for part in range(sub):
                    mean = jnp.mean(piece[:, part * tile : (part + 1) * tile], axis=1, keepdims=True)
                    means.append(jnp.broadcast_to(mean, (width, tile)))
                mean = jnp.concatenate(means, axis=1).astype(BF16)
                send_r[off, pl.ds(0, width), :] = (piece - mean.astype(F32)).astype(BF16)
                send_r[off, pl.ds(width, EXTRA), :] = dot_nt(chooser, mean).astype(BF16)
                r_copy(off).start()

            @pl.when(off == 0)
            def _():
                own_r[...] = piece

        for dist in range(2, chips):
            take_xc(dist)

        @pl.loop(0, chips)
        def _(zz):
            xcs_copy(other, zz).wait_recv()

        @pl.loop(0, cols)
        def _(step):
            off = lax.rem(step + 1, cols)
            at = window(lax.rem(c + off, cols))
            piece = dot(block[0, at, :], xc[p, 0]) + dot(block[1, at, :], xc[p, 1])

            @pl.when(off > 0)
            def _():
                lines = []
                for part in range(sub):
                    span = slice(part * tile, (part + 1) * tile)
                    mean = jnp.mean(piece[span], axis=0, keepdims=True).astype(BF16).astype(F32)
                    send_d[off, pl.ds(part * tile, tile), :] = (piece[span] - mean).astype(BF16)
                    lines.append(jnp.broadcast_to(mean, (EXTRA // sub, width)))
                send_d[off, pl.ds(nodes, EXTRA), :] = jnp.concatenate(lines, axis=0).astype(BF16)
                d_copy(off).start()

            @pl.when(off == 0)
            def _():
                own_d[...] = piece

        def spread(lines):
            reach = EXTRA // sub
            return jnp.concatenate(
                [
                    jnp.broadcast_to(lines[part * reach : part * reach + 1], (tile, width))
                    for part in range(sub)
                ],
                axis=0,
            )

        lines = jnp.zeros((EXTRA, width), F32)
        for off in range(1, cols):
            d_copy(off).wait_recv()
            own_d[...] += recv_d[p, off, pl.ds(0, nodes), :].astype(F32)
            lines = lines + recv_d[p, off, pl.ds(nodes, EXTRA), :].astype(F32)
        direct = own_d[...] + spread(lines)
        lines = jnp.zeros((EXTRA, width), F32)
        for off in range(1, chips):
            r_copy(off).wait_recv()
            own_r[...] += recv_r[p, off, pl.ds(0, width), :].astype(F32)
            lines = lines + recv_r[p, off, pl.ds(width, EXTRA), :].astype(F32)
        reverse = jnp.transpose(own_r[...]) + spread(lines)

        for off in range(1, cols):
            xr_copy(off).wait_send()
            d_copy(off).wait_send()
        for off in range(cols):
            xrs_copy(off, k).wait_send()
        for off in range(1, chips):
            r_copy(off).wait_send()

        @pl.loop(0, chips)
        def _(zz):
            xcs_copy(k, zz).wait_send()

        for dist in range(1, chips):

            @pl.when(jnp.logical_and(z - dist + 1 >= 0, z + 1 < chips))
            def _():
                xcr_copy(dist, z - dist + 1).wait_send()

            @pl.when(jnp.logical_and(z + dist - 1 < chips, z > 0))
            def _():
                xcl_copy(dist, z + dist - 1).wait_send()

        return direct, reverse

    @pl.loop(0, layers)
    def _(layer):
        hidden = hs[layer].astype(F32)
        first = (s_in[...] * hidden).astype(BF16)
        second_t = jnp.transpose(s_out[...] * hidden).astype(BF16)
        direct, reverse = exchange(layer, first, second_t)
        msg_in = (s_out[...] * direct).astype(BF16)
        msg_out = (s_in[...] * reverse).astype(BF16)
        ms_in[layer] = msg_in
        ms_out[layer] = msg_out
        preact = dot(msg_in, w_in[layer]) + dot(msg_out, w_out[layer])
        preact = preact + dot(hs[layer], w_self[layer]) + bias[pl.ds(layer, 1), :]
        zs[layer] = preact
        hs[layer + 1] = gelu(preact).astype(BF16)

    out_ref[...] = hs[layers]
    up[...] = cot[...].astype(F32)

    @pl.loop(0, layers)
    def _(step):
        layer = layers - 1 - step
        grad_z = (up[...] * gelu_slope(zs[layer])).astype(BF16)
        gz_ref[...] = grad_z
        back_in = jnp.transpose(s_out[...] * dot_nt(grad_z, w_in[layer])).astype(BF16)
        back_out = (s_in[...] * dot_nt(grad_z, w_out[layer])).astype(BF16)
        direct, reverse = exchange(layers + step, back_out, back_in)
        up[...] = (
            s_out[...] * direct + s_in[...] * reverse + dot_nt(gz_ref[...], w_self[layer])
        )
        grad_z = gz_ref[...]
        parts_ref[layer, pl.ds(0, width), :] = dot_tn(ms_in[layer], grad_z)
        parts_ref[layer, pl.ds(width, width), :] = dot_tn(ms_out[layer], grad_z)
        parts_ref[layer, pl.ds(2 * width, width), :] = dot_tn(hs[layer], grad_z)
        line = jnp.sum(grad_z.astype(F32), axis=0, keepdims=True)
        tail = parts_ref.shape[1] - 3 * width
        parts_ref[layer, pl.ds(3 * width, tail), :] = jnp.broadcast_to(line, (tail, width))

    gfeat_ref[...] = up[...]
    remote(block.at[other], sib_block, blk_sem, 0, sibling).wait_send()


def per_device(
    features,
    weight_in,
    weight_out,
    weight_self,
    layer_bias,
    out_degree,
    in_degree,
    tile_values,
    tile_pick,
    tile_count,
    cotangent,
):
    rows = lax.axis_size("row")
    cols = lax.axis_size("col")
    nodes, width = features.shape
    layers = weight_in.shape[0]
    slots, tile, unused = tile_values.shape
    chips = rows // 2
    tail = 64
    vmem = pl.BlockSpec(memory_space=pltpu.VMEM)
    smem = pl.BlockSpec(memory_space=pltpu.SMEM)
    sems = pltpu.SemaphoreType.DMA
    out, gfeat, parts = pl.pallas_call(
        functools.partial(kernel, rows, cols),
        out_shape=(
            jax.ShapeDtypeStruct((nodes, width), BF16),
            jax.ShapeDtypeStruct((nodes, width), F32),
            jax.ShapeDtypeStruct((layers, 3 * width + tail, width), F32),
        ),
        in_specs=[vmem] * 8 + [smem] * 2 + [pl.BlockSpec(memory_space=pl.ANY)],
        out_specs=(vmem, vmem, vmem),
        scratch_shapes=[
            pltpu.VMEM((2, cols * nodes, chips * nodes), BF16),
            pltpu.VMEM((cols * nodes, chips * nodes), BF16),
            pltpu.VMEM((slots, tile, tile), BF16),
            pltpu.VMEM((2, 2, chips * nodes, width), BF16),
            pltpu.VMEM((2, 2, width, cols * nodes), BF16),
            pltpu.VMEM((cols, nodes + EXTRA, width), BF16),
            pltpu.VMEM((2, cols, nodes + EXTRA, width), BF16),
            pltpu.VMEM((chips, width + EXTRA, nodes), BF16),
            pltpu.VMEM((2, chips, width + EXTRA, nodes), BF16),
            pltpu.VMEM((nodes, width), F32),
            pltpu.VMEM((width, nodes), F32),
            pltpu.VMEM((nodes, width), F32),
            pltpu.VMEM((nodes, width), F32),
            pltpu.VMEM((layers + 1, nodes, width), BF16),
            pltpu.VMEM((layers, nodes, width), BF16),
            pltpu.VMEM((layers, nodes, width), BF16),
            pltpu.VMEM((layers, nodes, width), F32),
            pltpu.VMEM((nodes, width), F32),
            pltpu.VMEM((nodes, width), BF16),
            sems((rows,)),
            sems((2, 1)),
            sems((2, 2, cols)),
            sems((2, 2, cols)),
            sems((2, 2, chips + 1)),
            sems((2, 2, chips + 1)),
            sems((2, 2, chips)),
            sems((2, 2, cols)),
            sems((2, 2, chips)),
        ],
        compiler_params=pltpu.CompilerParams(
            collective_id=0, has_side_effects=True, vmem_limit_bytes=63 * 1024 * 1024
        ),
    )(
        features,
        weight_in,
        weight_out,
        weight_self,
        layer_bias,
        out_degree.reshape(1, nodes),
        in_degree.reshape(1, nodes),
        cotangent,
        tile_pick,
        tile_count,
        tile_values,
    )
    total = parts.reshape(-1, width)
    total = lax.psum_scatter(total, "row", scatter_dimension=0, tiled=True)
    total = lax.psum_scatter(total, "col", scatter_dimension=0, tiled=True)
    total = lax.all_gather(total, ("row", "col"), axis=0, tiled=True)
    total = total.reshape(layers, -1, width)
    return (
        out,
        gfeat,
        total[:, :width],
        total[:, width : 2 * width],
        total[:, 2 * width : 3 * width],
        total[:, 3 * width],
    )


def solution(mesh):
    return jax.shard_map(
        per_device,
        mesh=mesh,
        in_specs=(
            P(("row", "col"), None),
            P(),
            P(),
            P(),
            P(),
            P(("row", "col")),
            P(("row", "col")),
            P(("row", "col"), None, None),
            P(("row", "col")),
            P(("row", "col")),
            P(("row", "col"), None),
        ),
        out_specs=(P(("row", "col"), None), P(("row", "col"), None), P(), P(), P(), P()),
        check_vma=False,
    )
```

time: 430 us -> 271 us (0.63)
  waiting for transfers between devices: 280 us -> 90.7 us
  Pallas kernels: 0 us -> 134 us
  matrix products: 42.9 us -> 0 us
  blocking collectives: 52.4 us -> 21.5 us
  other arithmetic: 13.8 us -> 0 us
  starting transfers between devices: 14.7 us -> 2.55 us
  local copies, waits for them, and re-layouts: 11.1 us -> 6.06 us
    pallas_call x0 -> x1, Pallas kernels: none -> 134 us  [per_device(): pl.pallas_call(functools.partial(kernel, rows, cols), out_shape=(jax.Shap...]
    reduce_scatter x5 -> x0, waiting for transfers between devices: 103 us -> none  [the longest x4 96.2 us: forward_messages(): lax.psum_scatter(reverse, 'row', scatter_dimension=0, tiled=True)]
    all_gather x4 -> x0, waiting for transfers between devices: 54.6 us -> none  [forward_messages(): column_rows = lax.all_gather(first, 'row', axis=0, tiled=True)]
    all_gather x4 -> x0, blocking collectives: 52.4 us -> none  [forward_messages(): row_rows = lax.all_gather(second, 'col', axis=0, tiled=True)]
    dot_general x22 -> x0, matrix products: 42.9 us -> none  [the longest x4 18.3 us: forward_messages(): direct = jnp.dot(block, column_rows, preferred_element_type=jnp.float32)]
    all_to_all x4 -> x0, waiting for transfers between devices: 31.5 us -> none  [forward_messages(): pieces = lax.all_to_all(pieces, 'col', 0, 0, tiled=True)]
    unnamed x0 -> x1, blocking collectives: none -> 21.5 us
    all_to_all x4 -> x0, starting transfers between devices: 14 us -> none  [forward_messages(): pieces = lax.all_to_all(pieces, 'col', 0, 0, tiled=True)]
  transfers between devices with their start and end apart: 15 -> 3, of which waited for: 14 -> 3; matrix products, arithmetic and copies ran while one was open for 10% -> 0% of each run, Pallas kernels for 0% -> 0%
where the time goes in v1:
time: 271 us; the launch traced here: 270 us
  Pallas kernels  134 us (49%)
  waiting for transfers between devices  90.7 us (33%)
  blocking collectives  21.5 us (8%)
  between operations  15.4 us (6%)
  local copies, waits for them, and re-layouts  6.06 us (2%)
    pallas_call x1, Pallas kernels, per_device(): pl.pallas_call(functools.partial(kernel, rows, cols), out_shape=(jax.Shap...  134 us
    all_gather x1, waiting for transfers between devices, per_device(): total = lax.all_gather(total, ('row', 'col'), axis=0, tiled=True)  57.7 us
    reduce_scatter x1, waiting for transfers between devices, per_device(): total = lax.psum_scatter(total, 'row', scatter_dimension=0, tiled=True)  32.6 us
    unnamed x1, blocking collectives  21.5 us
  transfers between devices with their start and end apart: 3, of which 3 were waited for; matrix products, arithmetic and copies ran while one was open for 0% of the time, Pallas kernels for 0%

profile of v1, /device:TPU:0, one launch (start us, length us, event | category | flops | bytes accessed | tf_op | source)
XLA Modules:
  0.0 270.3 jit_solution(6960509178576734974)
XLA Ops:
  7.2 0.0 reduce-scatter.4.cloned.1.call-start
  7.9 134.1 %shard_map.154 = (bf16[256,256]{1,0:T(8,128)(2,1)}, f32[256,256]{1,0:T(8,128)}, f32[2,832,256]{2,1,0:T(8,128)}) custom-call(bf16[256,256]{1,0:T(8,128)(2,1)} %feat.1, bf16[2,256,256]{2,1,0:T(8,128)(2,1)} %w_in.1, bf16[2,256,256]{2,1,0:T(8,128)(2,1)} %w_out.1, bf16[2,256,256]{2,1,0:T(8,128)(2,1)} %w_self.1, f32[2,256]{1,0:T(2,128)} %bias.1, ...), custom_call_target="tpu_custom_call" | custom-call | tf_op jit(solution)/shard_map/pallas_call | solution.py:429
  141.9 0.0 copy-start.2
  142.0 0.0 reduce-scatter.4.cloned.1.call-update
  142.0 0.0 all-gather.3.cloned.1.call-start
  142.0 32.6 %reduce-scatter.4.cloned.1.call-done = f32[208,256]{1,0:T(8,128)} async-done(((f32[1664,256]{1,0:T(8,128)}), f32[208,256]{1,0:T(8,128)}) %reduce-scatter.4.cloned.1.call-update) | async-done | bytes 213008 | tf_op jit(solution)/shard_map/reduce_scatter | solution.py:485
  174.6 21.5 %fusion = f32[64,256]{1,0:T(8,128)S(1)} fusion(f32[208,256]{1,0:T(8,128)} %reduce-scatter.4.cloned.1.call-done), kind=kCustom, calls=%all-reduce-scatter | all-reduce-scatter fusion | flops 65537 | bytes 279040
  196.1 2.5 collective-permute-start
  198.6 0.0 copy-done.2
  198.6 0.6 dynamic-slice.4
  199.8 0.4 collective-permute-done
  200.2 0.2 concatenate
  200.4 0.6 dynamic-slice_bitcast_fusion
  201.0 0.0 all-gather.3.cloned.1.call-update
  201.1 57.7 %all-gather.3.cloned.1.call-done = f32[32,52,256]{2,1,0:T(8,128)} async-done(((f32[1,52,256]{2,1,0:T(8,128)}), f32[32,52,256]{2,1,0:T(8,128)}) %all-gather.3.cloned.1.call-update) | async-done | bytes 1703952 | tf_op jit(solution)/shard_map/all_gather | solution.py:487
  258.8 1.5 reshape.27
  260.3 0.0 copy-start.1
  260.3 0.0 copy-start
  260.3 1.2 fusion.1
  261.5 0.6 copy.22
  262.1 0.0 copy-done.1
  262.1 0.7 copy.26
  262.7 0.0 copy-done
  262.8 0.7 copy.27
  (2 shorter events, 0.0 us)
Async XLA Ops:
  7.2 167.4 %reduce-scatter.4.cloned.1.call-start = ((), (), s32[]{:S(2)}) async-start(), calls=%async_computation.1 | async-start | bytes 1916928 | tf_op jit(solution)/shard_map/reduce_scatter | solution.py:485
  141.9 56.6 %copy-start.2 = (u32[32]{0:T(128)S(1)}, u32[32]{0:T(128)}, u32[]{:S(2)}) copy-start(u32[32]{0:T(128)} %constant.3) | copy-start | bytes 388
  142.0 116.8 %all-gather.3.cloned.1.call-start = ((), (), s32[]{:S(2)}) async-start(), calls=%async_computation.2 | async-start | bytes 1892352 | tf_op jit(solution)/shard_map/all_gather | solution.py:487
  196.1 4.1 %collective-permute-start = (f32[36,256]{1,0:T(8,128)S(1)}, f32[36,256]{1,0:T(8,128)S(1)}, u32[]{:S(2)}, u32[]{:S(2)}) collective-permute-start(f32[36,256]{1,0:T(8,128)S(1)} %slice.20), channel_id=1, source_target_pairs={{0,1},{1,2},{2,3},{4,5},{5,6},{6,7},{8,9},{9,10},{10,11},{12,13},{... | collective-permute-start | bytes 110600
  260.3 1.8 copy-start.1
  260.3 2.4 copy-start
Sparse Core Ops, SparseCore 0:
  142.1 32.4 reduce-scatter.3
  201.2 57.5 all-gather.2

commit v2 on v1

--- a/solution.py
+++ b/solution.py
@@ -52,7 +52,7 @@
     tiles,
     out_ref,
     gfeat_ref,
-    parts_ref,
+    grads_ref,
     block,
     sib_block,
     staged,
@@ -72,6 +72,14 @@
     zs,
     up,
     gz_ref,
+    g_full,
+    g_send,
+    g_recv,
+    gc_send,
+    gc_recv,
+    gz_send,
+    gz_recv,
+    g_all,
     tile_sem,
     blk_sem,
     xr_sem,
@@ -81,6 +89,12 @@
     xcs_sem,
     d_sem,
     r_sem,
+    gs_sem,
+    gc_sem,
+    gz_sem,
+    az_sem,
+    ac_sem,
+    as_sem,
 ):
     chips = rows // 2
     nodes, width = feat.shape
@@ -173,8 +187,12 @@
     def window(zz):
         return pl.ds(pl.multiple_of(zz * nodes, nodes), nodes)
 
-    def exchange(stage, first, second_t):
+    def exchange(stage, first, second_t, points=()):
         p = lax.rem(stage, 2)
+
+        def visit(number):
+            if points:
+                points[number]()
 
         def xr_copy(off):
             mine = xr.at[p, k, :, window(c)]
@@ -223,6 +241,8 @@
         @pl.when(stage == 0)
         def _():
             build()
+
+        visit(0)
 
         def take_xr(off):
             source = lax.rem(c + cols - off, cols)
@@ -287,6 +307,8 @@
             def _():
                 own_r[...] = piece
 
+        visit(1)
+
         for dist in range(2, chips):
             take_xc(dist)
 
@@ -314,6 +336,8 @@
             @pl.when(off == 0)
             def _():
                 own_d[...] = piece
+
+        visit(2)
 
         def spread(lines):
             reach = EXTRA // sub
@@ -331,12 +355,14 @@
             own_d[...] += recv_d[p, off, pl.ds(0, nodes), :].astype(F32)
             lines = lines + recv_d[p, off, pl.ds(nodes, EXTRA), :].astype(F32)
         direct = own_d[...] + spread(lines)
+        visit(3)
         lines = jnp.zeros((EXTRA, width), F32)
         for off in range(1, chips):
             r_copy(off).wait_recv()
             own_r[...] += recv_r[p, off, pl.ds(0, width), :].astype(F32)
             lines = lines + recv_r[p, off, pl.ds(width, EXTRA), :].astype(F32)
         reverse = jnp.transpose(own_r[...]) + spread(lines)
+        visit(4)
 
         for off in range(1, cols):
             xr_copy(off).wait_send()
@@ -361,6 +387,108 @@
                 xcl_copy(dist, z + dist - 1).wait_send()
 
         return direct, reverse
+
+    half = g_send.shape[0]
+    depth = gz_send.shape[1]
+
+    def reduction(layer, p):
+        def to_sibling():
+            return remote(g_send, g_recv.at[p], gs_sem, 0, sibling, p)
+
+        def to_col(off):
+            target = at_col(lax.rem(c + off, cols))
+            return remote(gc_send.at[off], gc_recv.at[p, off], gc_sem, off, target, p)
+
+        def to_chip(off):
+            target = at_chip(lax.rem(z + off, chips))
+            return remote(gz_send.at[off], gz_recv.at[p, off], gz_sem, off, target, p)
+
+        def slot(kk, cc, zz, count):
+            start = pl.multiple_of(((kk * cols + cc) * chips + zz) * depth, depth)
+            return g_all.at[layer, pl.ds(start, count * depth), :]
+
+        def spread_chip(off, zz):
+            view = slot(k, c, zz, 1)
+            return remote(view, view, az_sem, off, at_chip(lax.rem(z + off, chips)), p)
+
+        def spread_col(off, cc):
+            view = slot(k, cc, 0, chips)
+            return remote(view, view, ac_sem, off, at_col(lax.rem(c + off, cols)), p)
+
+        def spread_sibling(kk, cc):
+            view = slot(kk, cc, 0, chips)
+            return remote(view, view, as_sem, cc, sibling, p)
+
+        def mine():
+            return pl.ds(pl.multiple_of(k * half, half), half)
+
+        def block_of(cc):
+            return pl.ds(pl.multiple_of(k * half + cc * (chips * depth), depth), chips * depth)
+
+        def share_of(zz):
+            start = k * half + c * (chips * depth) + zz * depth
+            return pl.ds(pl.multiple_of(start, depth), depth)
+
+        def start():
+            width = gz_ref.shape[1]
+            grad = gz_ref[...]
+            for at, left in enumerate((ms_in, ms_out, hs)):
+                g_full[pl.ds(at * width, width), :] = dot_tn(left[layer], grad)
+            line = jnp.sum(grad.astype(F32), axis=0, keepdims=True)
+            g_full[pl.ds(3 * width, 8), :] = jnp.broadcast_to(line, (8, width))
+            theirs = pl.ds(pl.multiple_of(other * half, half), half)
+            g_send[...] = g_full[theirs, :].astype(BF16)
+            to_sibling().start()
+
+        def over_cols():
+            to_sibling().wait_recv()
+            g_full[mine(), :] += g_recv[p].astype(F32)
+            for off in range(1, cols):
+                gc_send[off] = g_full[block_of(lax.rem(c + off, cols)), :].astype(BF16)
+                to_col(off).start()
+
+        def over_chips():
+            for off in range(1, cols):
+                to_col(off).wait_recv()
+                g_full[block_of(c), :] += gc_recv[p, off].astype(F32)
+            for off in range(1, chips):
+                gz_send[off] = g_full[share_of(lax.rem(z + off, chips)), :].astype(BF16)
+                to_chip(off).start()
+
+        def back_chips():
+            for off in range(1, chips):
+                to_chip(off).wait_recv()
+                g_full[share_of(z), :] += gz_recv[p, off].astype(F32)
+            at = pl.multiple_of(((k * cols + c) * chips + z) * depth, depth)
+            g_all[layer, pl.ds(at, depth), :] = g_full[share_of(z), :].astype(BF16)
+            for off in range(1, chips):
+                spread_chip(off, z).start()
+
+        def back_cols():
+            for off in range(1, chips):
+                spread_chip(off, lax.rem(z + chips - off, chips)).wait_recv()
+            for off in range(1, cols):
+                spread_col(off, c).start()
+            spread_sibling(k, c).start()
+            for off in range(1, cols):
+                source = lax.rem(c + cols - off, cols)
+                spread_col(off, source).wait_recv()
+                spread_sibling(k, source).start()
+            for off in range(cols):
+                spread_sibling(other, lax.rem(c + off, cols)).wait_recv()
+            to_sibling().wait_send()
+            for off in range(1, cols):
+                to_col(off).wait_send()
+                spread_col(off, c).wait_send()
+            for off in range(1, chips):
+                to_chip(off).wait_send()
+                spread_chip(off, z).wait_send()
+            for off in range(cols):
+                spread_sibling(k, lax.rem(c + off, cols)).wait_send()
+
+        return start, over_cols, over_chips, back_chips, back_cols
+
+    g_full[...] = jnp.zeros(g_full.shape, F32)
 
     @pl.loop(0, layers)
     def _(layer):
@@ -387,18 +515,14 @@
         gz_ref[...] = grad_z
         back_in = jnp.transpose(s_out[...] * dot_nt(grad_z, w_in[layer])).astype(BF16)
         back_out = (s_in[...] * dot_nt(grad_z, w_out[layer])).astype(BF16)
-        direct, reverse = exchange(layers + step, back_out, back_in)
+        direct, reverse = exchange(
+            layers + step, back_out, back_in, reduction(layer, lax.rem(layers + step, 2))
+        )
         up[...] = (
             s_out[...] * direct + s_in[...] * reverse + dot_nt(gz_ref[...], w_self[layer])
         )
-        grad_z = gz_ref[...]
-        parts_ref[layer, pl.ds(0, width), :] = dot_tn(ms_in[layer], grad_z)
-        parts_ref[layer, pl.ds(width, width), :] = dot_tn(ms_out[layer], grad_z)
-        parts_ref[layer, pl.ds(2 * width, width), :] = dot_tn(hs[layer], grad_z)
-        line = jnp.sum(grad_z.astype(F32), axis=0, keepdims=True)
-        tail = parts_ref.shape[1] - 3 * width
-        parts_ref[layer, pl.ds(3 * width, tail), :] = jnp.broadcast_to(line, (tail, width))
-
+
+    grads_ref[...] = g_all[...]
     gfeat_ref[...] = up[...]
     remote(block.at[other], sib_block, blk_sem, 0, sibling).wait_send()
 
@@ -422,16 +546,17 @@
     layers = weight_in.shape[0]
     slots, tile, unused = tile_values.shape
     chips = rows // 2
-    tail = 64
+    depth = -(-(3 * width + 8) // (rows * cols * 16)) * 16
+    total = rows * cols * depth
     vmem = pl.BlockSpec(memory_space=pltpu.VMEM)
     smem = pl.BlockSpec(memory_space=pltpu.SMEM)
     sems = pltpu.SemaphoreType.DMA
-    out, gfeat, parts = pl.pallas_call(
+    out, gfeat, grads = pl.pallas_call(
         functools.partial(kernel, rows, cols),
         out_shape=(
             jax.ShapeDtypeStruct((nodes, width), BF16),
             jax.ShapeDtypeStruct((nodes, width), F32),
-            jax.ShapeDtypeStruct((layers, 3 * width + tail, width), F32),
+            jax.ShapeDtypeStruct((layers, total, width), BF16),
         ),
         in_specs=[vmem] * 8 + [smem] * 2 + [pl.BlockSpec(memory_space=pl.ANY)],
         out_specs=(vmem, vmem, vmem),
@@ -455,6 +580,14 @@
             pltpu.VMEM((layers, nodes, width), F32),
             pltpu.VMEM((nodes, width), F32),
             pltpu.VMEM((nodes, width), BF16),
+            pltpu.VMEM((total, width), F32),
+            pltpu.VMEM((total // 2, width), BF16),
+            pltpu.VMEM((2, total // 2, width), BF16),
+            pltpu.VMEM((cols, chips * depth, width), BF16),
+            pltpu.VMEM((2, cols, chips * depth, width), BF16),
+            pltpu.VMEM((chips, depth, width), BF16),
+            pltpu.VMEM((2, chips, depth, width), BF16),
+            pltpu.VMEM((layers, total, width), BF16),
             sems((rows,)),
             sems((2, 1)),
             sems((2, 2, cols)),
@@ -464,6 +597,12 @@
             sems((2, 2, chips)),
             sems((2, 2, cols)),
             sems((2, 2, chips)),
+            sems((2, 2, 1)),
+            sems((2, 2, cols)),
+            sems((2, 2, chips)),
+            sems((2, 2, chips)),
+            sems((2, 2, cols)),
+            sems((2, 2, cols)),
         ],
         compiler_params=pltpu.CompilerParams(
             collective_id=0, has_side_effects=True, vmem_limit_bytes=63 * 1024 * 1024
@@ -481,18 +620,14 @@
         tile_count,
         tile_values,
     )
-    total = parts.reshape(-1, width)
-    total = lax.psum_scatter(total, "row", scatter_dimension=0, tiled=True)
-    total = lax.psum_scatter(total, "col", scatter_dimension=0, tiled=True)
-    total = lax.all_gather(total, ("row", "col"), axis=0, tiled=True)
-    total = total.reshape(layers, -1, width)
+    grads = grads.astype(F32)
     return (
         out,
         gfeat,
-        total[:, :width],
-        total[:, width : 2 * width],
-        total[:, 2 * width : 3 * width],
-        total[:, 3 * width],
+        grads[:, :width],
+        grads[:, width : 2 * width],
+        grads[:, 2 * width : 3 * width],
+        grads[:, 3 * width],
     )
 
 

time: 271 us -> 164 us (0.61)
  waiting for transfers between devices: 90.7 us -> 0 us
  blocking collectives: 21.5 us -> 0 us
  Pallas kernels: 134 us -> 155 us
  between operations: 15.4 us -> 1.29 us
    all_gather x1 -> x0, waiting for transfers between devices: 57.7 us -> none  [per_device(): total = lax.all_gather(total, ('row', 'col'), axis=0, tiled=True)]
    reduce_scatter x1 -> x0, waiting for transfers between devices: 32.6 us -> none  [per_device(): total = lax.psum_scatter(total, 'row', scatter_dimension=0, tiled=True)]
    unnamed x1 -> x0, blocking collectives: 21.5 us -> none
    pallas_call x1, Pallas kernels: 134 us -> 155 us  [per_device(): pl.pallas_call(functools.partial(kernel, rows, cols), out_shape=(jax.Shap...]
  transfers between devices with their start and end apart: 3 -> 0, of which waited for: 3 -> 0; matrix products, arithmetic and copies ran while one was open for 0% -> 0% of each run, Pallas kernels for 0% -> 0%
where the time goes in v2:
time: 164 us; the launch traced here: 163 us
  Pallas kernels  155 us (95%)
  local copies, waits for them, and re-layouts  6.81 us (4%)
    pallas_call x1, Pallas kernels, per_device(): pl.pallas_call(functools.partial(kernel, rows, cols), out_shape=(jax.Shap...  155 us
    unnamed x3, local copies, waits for them, and re-layouts  3.82 us

profile of v2, /device:TPU:0, one launch (start us, length us, event | category | flops | bytes accessed | tf_op | source)
XLA Modules:
  0.0 162.7 jit_solution(12610517238894591515)
XLA Ops:
  1.3 154.6 %shard_map.154 = (bf16[256,256]{1,0:T(8,128)(2,1)}, f32[256,256]{1,0:T(8,128)}, bf16[2,1024,256]{2,1,0:T(8,128)(2,1)}) custom-call(bf16[256,256]{1,0:T(8,128)(2,1)} %feat.1, bf16[2,256,256]{2,1,0:T(8,128)(2,1)} %w_in.1, bf16[2,256,256]{2,1,0:T(8,128)(2,1)} %w_out.1, bf16[2,256,256]{2,1,0:T(8,128)(2,1)} %w_self.1, f32[2,256]{1,0:T(2,128)} %bias.1, ...), custom_call_target="tpu_custom_call" | custom-call | tf_op jit(solution)/shard_map/pallas_call | solution.py:554
  155.9 2.3 %fusion = (f32[2,256,256]{2,1,0:T(8,128)}, f32[2,256,256]{2,1,0:T(8,128)}, f32[2,256,256]{2,1,0:T(8,128)}) fusion(bf16[2,1024,256]{2,1,0:T(8,128)(2,1)} %get-tuple-element.11), kind=kLoop, calls=%fused_computation.1 | loop fusion | bytes 3145728 | tf_op jit(solution)/shard_map/slice | solution.py:629
  158.2 0.7 slice.19
  158.9 0.6 copy.19
  159.4 1.6 copy.23
  161.0 1.7 %copy.24 = f32[256,256]{1,0:T(8,128)} copy(f32[256,256]{1,0:T(8,128)} %get-tuple-element.22) | data formatting | bytes 524288

commit v3 on v2

--- a/solution.py
+++ b/solution.py
@@ -64,6 +64,8 @@
     recv_r,
     own_d,
     own_r,
+    sums_d,
+    sums_r,
     s_in,
     s_out,
     hs,
@@ -101,6 +103,7 @@
     layers = w_in.shape[0]
     tile = staged.shape[1]
     sub = nodes // tile
+    part_width = width // 2
     slots = staged.shape[0]
     per = slots // (rows * cols)
     row = lax.axis_index("row")
@@ -194,49 +197,59 @@
             if points:
                 points[number]()
 
-        def xr_copy(off):
-            mine = xr.at[p, k, :, window(c)]
-            return remote(mine, mine, xr_sem, off, at_col(lax.rem(c + off, cols)), p)
-
-        def xrs_copy(off, kk):
-            view = xr.at[p, kk, :, window(lax.rem(c + cols - off, cols))]
-            return remote(view, view, xrs_sem, off, sibling, p)
-
-        def xc_view(kk, zz):
-            return xc.at[p, kk, window(zz), :]
-
-        def xcr_copy(dist, zz):
-            return remote(xc_view(k, zz), xc_view(k, zz), xcr_sem, dist, at_chip(z + 1), p)
-
-        def xcl_copy(dist, zz):
-            return remote(xc_view(k, zz), xc_view(k, zz), xcl_sem, dist, at_chip(z - 1), p)
-
-        def xcs_copy(kk, zz):
-            return remote(xc_view(kk, zz), xc_view(kk, zz), xcs_sem, zz, sibling, p)
-
-        def d_copy(off):
+        def xr_view(h, kk, cc):
+            return xr.at[p, h, kk, :, window(cc)]
+
+        def xr_copy(h, off):
+            mine = xr_view(h, k, c)
+            return remote(mine, mine, xr_sem, h * cols + off, at_col(lax.rem(c + off, cols)), p)
+
+        def xrs_copy(h, off, kk):
+            view = xr_view(h, kk, lax.rem(c + cols - off, cols))
+            return remote(view, view, xrs_sem, h * cols + off, sibling, p)
+
+        def xc_view(h, kk, zz):
+            return xc.at[p, h, kk, window(zz), :]
+
+        def xcr_copy(h, dist, zz):
+            view = xc_view(h, k, zz)
+            return remote(view, view, xcr_sem, h * (chips + 1) + dist, at_chip(z + 1), p)
+
+        def xcl_copy(h, dist, zz):
+            view = xc_view(h, k, zz)
+            return remote(view, view, xcl_sem, h * (chips + 1) + dist, at_chip(z - 1), p)
+
+        def xcs_copy(h, kk, zz):
+            view = xc_view(h, kk, zz)
+            return remote(view, view, xcs_sem, h * chips + zz, sibling, p)
+
+        def d_copy(h, off):
             target = at_col(lax.rem(c + off, cols))
-            return remote(send_d.at[off], recv_d.at[p, off], d_sem, off, target, p)
-
-        def r_copy(off):
-            target = at_chip(lax.rem(z + off, chips))
-            return remote(send_r.at[off], recv_r.at[p, off], r_sem, off, target, p)
-
-        xr[p, k, :, window(c)] = second_t
-        xc[p, k, window(z), :] = first
-        for off in range(1, cols):
-            xr_copy(off).start()
-        xrs_copy(0, k).start()
-
-        @pl.when(z + 1 < chips)
-        def _():
-            xcr_copy(1, z).start()
-
-        @pl.when(z > 0)
-        def _():
-            xcl_copy(1, z).start()
-
-        xcs_copy(k, z).start()
+            return remote(send_d.at[h, off], recv_d.at[p, h, off], d_sem, h * cols + off, target, p)
+
+        def r_copy(h, way, dest):
+            target = at_chip(z + 1 if way == 0 else z - 1)
+            landing = recv_r.at[p, h, way, dest]
+            return remote(send_r.at[h, dest], landing, r_sem, (h * 2 + way) * chips + dest, target, p)
+
+        for h in range(2):
+            span = slice(h * part_width, (h + 1) * part_width)
+            xr[p, h, k, :, window(c)] = second_t[span, :]
+            xc[p, h, k, window(z), :] = first[:, span]
+        for h in range(2):
+            for off in range(1, cols):
+                xr_copy(h, off).start()
+
+            @pl.when(z + 1 < chips)
+            def _():
+                xcr_copy(h, 1, z).start()
+
+            @pl.when(z > 0)
+            def _():
+                xcl_copy(h, 1, z).start()
+
+            xrs_copy(h, 0, k).start()
+            xcs_copy(h, k, z).start()
 
         @pl.when(stage == 0)
         def _():
@@ -244,149 +257,208 @@
 
         visit(0)
 
-        def take_xr(off):
+        def take_xr(h, off):
             source = lax.rem(c + cols - off, cols)
-            view = xr.at[p, k, :, window(source)]
-            remote(view, view, xr_sem, off, at_col(source), p).wait_recv()
-            xrs_copy(off, k).start()
-
-        def take_xc(dist):
+            view = xr_view(h, k, source)
+            remote(view, view, xr_sem, h * cols + off, at_col(source), p).wait_recv()
+            xrs_copy(h, off, k).start()
+
+        def take_xc(h, dist):
             @pl.when(z - dist >= 0)
             def _():
-                xcr_copy(dist, z - dist).wait_recv()
+                xcr_copy(h, dist, z - dist).wait_recv()
 
                 @pl.when(z + 1 < chips)
                 def _():
-                    xcr_copy(dist + 1, z - dist).start()
-
-                xcs_copy(k, z - dist).start()
+                    xcr_copy(h, dist + 1, z - dist).start()
+
+                xcs_copy(h, k, z - dist).start()
 
             @pl.when(z + dist < chips)
             def _():
-                xcl_copy(dist, z + dist).wait_recv()
+                xcl_copy(h, dist, z + dist).wait_recv()
 
                 @pl.when(z > 0)
                 def _():
-                    xcl_copy(dist + 1, z + dist).start()
-
-                xcs_copy(k, z + dist).start()
-
-        for off in range(1, cols):
-            take_xr(off)
-            if off == 1:
-                take_xc(1)
-        for off in range(cols):
-            xrs_copy(off, other).wait_recv()
-
-        @pl.when(stage == 0)
-        def _():
-            remote(block.at[other], sib_block, blk_sem, 0, sibling).wait_recv()
-
+                    xcl_copy(h, dist + 1, z + dist).start()
+
+                xcs_copy(h, k, z + dist).start()
+
+        reach = EXTRA // sub
         lanes = lax.broadcasted_iota(jnp.int32, (EXTRA, nodes), 1)
-        groups = lax.broadcasted_iota(jnp.int32, (EXTRA, nodes), 0) // (EXTRA // sub)
-        chooser = jnp.where(lanes == groups * tile, 1.0, 0.0).astype(BF16)
-
-        @pl.loop(0, chips)
-        def _(step):
-            off = lax.rem(step + 1, chips)
-            at = window(lax.rem(z + off, chips))
-            piece = dot(xr[p, k], block[k, :, at]) + dot(xr[p, other], sib_block[:, at])
-
-            @pl.when(off > 0)
+        lines = lax.broadcasted_iota(jnp.int32, (EXTRA, nodes), 0)
+        chooser = jnp.where(lanes == (lines // reach) * tile, 1.0, 0.0).astype(BF16)
+        spreader = jnp.where(lines == (lanes // tile) * reach, 1.0, 0.0).astype(BF16)
+
+        def reverse_products(h):
+            for off in range(cols):
+                xrs_copy(h, off, other).wait_recv()
+            if h == 0:
+
+                @pl.when(stage == 0)
+                def _():
+                    remote(block.at[other], sib_block, blk_sem, 0, sibling).wait_recv()
+
+            @pl.loop(0, chips)
+            def _(dest):
+                at = window(dest)
+                own_r[h, dest] = dot(xr[p, h, k], block[k, :, at]) + dot(
+                    xr[p, h, other], sib_block[:, at]
+                )
+
+        def r_send(h, way, dest, total):
+            means = []
+            for part in range(sub):
+                mean = jnp.mean(total[:, part * tile : (part + 1) * tile], axis=1, keepdims=True)
+                means.append(jnp.broadcast_to(mean, (part_width, tile)))
+            mean = jnp.concatenate(means, axis=1).astype(BF16)
+            send_r[h, dest, pl.ds(0, part_width), :] = (total - mean.astype(F32)).astype(BF16)
+            send_r[h, dest, pl.ds(part_width, EXTRA), pl.ds(0, part_width)] = dot_nt(
+                chooser, mean
+            ).astype(BF16)
+            r_copy(h, way, dest).start()
+
+        def r_take(h, way, dest):
+            r_copy(h, way, dest).wait_recv()
+            mean = recv_r[p, h, way, dest, pl.ds(part_width, EXTRA), pl.ds(0, part_width)]
+            rest = recv_r[p, h, way, dest, pl.ds(0, part_width), :].astype(F32)
+            return rest + dot_tn(mean, spreader)
+
+        def r_first(h):
+            for dist in range(chips - 1, 0, -1):
+
+                @pl.when(z == 0)
+                def _():
+                    r_send(h, 0, dist, own_r[h, dist])
+
+                @pl.when(z == chips - 1)
+                def _():
+                    r_send(h, 1, chips - 1 - dist, own_r[h, chips - 1 - dist])
+
+        def r_relay(h, dist):
+            @pl.when(jnp.logical_and(z > 0, z + dist < chips))
             def _():
-                means = []
-                for part in range(sub):
-                    mean = jnp.mean(piece[:, part * tile : (part + 1) * tile], axis=1, keepdims=True)
-                    means.append(jnp.broadcast_to(mean, (width, tile)))
-                mean = jnp.concatenate(means, axis=1).astype(BF16)
-                send_r[off, pl.ds(0, width), :] = (piece - mean.astype(F32)).astype(BF16)
-                send_r[off, pl.ds(width, EXTRA), :] = dot_nt(chooser, mean).astype(BF16)
-                r_copy(off).start()
-
-            @pl.when(off == 0)
+                r_send(h, 0, z + dist, own_r[h, z + dist] + r_take(h, 0, z + dist))
+
+            @pl.when(jnp.logical_and(z < chips - 1, z - dist >= 0))
             def _():
-                own_r[...] = piece
-
-        visit(1)
-
-        for dist in range(2, chips):
-            take_xc(dist)
-
-        @pl.loop(0, chips)
-        def _(zz):
-            xcs_copy(other, zz).wait_recv()
-
-        @pl.loop(0, cols)
-        def _(step):
-            off = lax.rem(step + 1, cols)
-            at = window(lax.rem(c + off, cols))
-            piece = dot(block[0, at, :], xc[p, 0]) + dot(block[1, at, :], xc[p, 1])
-
-            @pl.when(off > 0)
-            def _():
-                lines = []
-                for part in range(sub):
-                    span = slice(part * tile, (part + 1) * tile)
-                    mean = jnp.mean(piece[span], axis=0, keepdims=True).astype(BF16).astype(F32)
-                    send_d[off, pl.ds(part * tile, tile), :] = (piece[span] - mean).astype(BF16)
-                    lines.append(jnp.broadcast_to(mean, (EXTRA // sub, width)))
-                send_d[off, pl.ds(nodes, EXTRA), :] = jnp.concatenate(lines, axis=0).astype(BF16)
-                d_copy(off).start()
-
-            @pl.when(off == 0)
-            def _():
-                own_d[...] = piece
-
-        visit(2)
+                r_send(h, 1, z - dist, own_r[h, z - dist] + r_take(h, 1, z - dist))
+
+        def direct_products(h):
+            @pl.loop(0, chips)
+            def _(zz):
+                xcs_copy(h, other, zz).wait_recv()
+
+            @pl.loop(0, cols)
+            def _(step):
+                off = lax.rem(step + 1, cols)
+                at = window(lax.rem(c + off, cols))
+                piece = dot(block[0, at, :], xc[p, h, 0]) + dot(block[1, at, :], xc[p, h, 1])
+
+                @pl.when(off > 0)
+                def _():
+                    heads = []
+                    for part in range(sub):
+                        span = slice(part * tile, (part + 1) * tile)
+                        mean = jnp.mean(piece[span], axis=0, keepdims=True).astype(BF16).astype(F32)
+                        send_d[h, off, pl.ds(part * tile, tile), :] = (piece[span] - mean).astype(BF16)
+                        heads.append(jnp.broadcast_to(mean, (reach, part_width)))
+                    send_d[h, off, pl.ds(nodes, EXTRA), :] = jnp.concatenate(heads, axis=0).astype(BF16)
+                    d_copy(h, off).start()
+
+                @pl.when(off == 0)
+                def _():
+                    own_d[h] = piece
 
         def spread(lines):
-            reach = EXTRA // sub
             return jnp.concatenate(
                 [
-                    jnp.broadcast_to(lines[part * reach : part * reach + 1], (tile, width))
+                    jnp.broadcast_to(lines[part * reach : part * reach + 1], (tile, part_width))
                     for part in range(sub)
                 ],
                 axis=0,
             )
 
-        lines = jnp.zeros((EXTRA, width), F32)
+        def direct_total(h):
+            total = own_d[h]
+            heads = jnp.zeros((EXTRA, part_width), F32)
+            for off in range(1, cols):
+                d_copy(h, off).wait_recv()
+                total = total + recv_d[p, h, off, pl.ds(0, nodes), :].astype(F32)
+                heads = heads + recv_d[p, h, off, pl.ds(nodes, EXTRA), :].astype(F32)
+            sums_d[:, pl.ds(h * part_width, part_width)] = total + spread(heads)
+
+        def reverse_total(h):
+            @pl.when(z > 0)
+            def _():
+                own_r[h, z] += r_take(h, 0, z)
+
+            @pl.when(z < chips - 1)
+            def _():
+                own_r[h, z] += r_take(h, 1, z)
+
+            sums_r[:, pl.ds(h * part_width, part_width)] = jnp.transpose(own_r[h, z])
+
         for off in range(1, cols):
-            d_copy(off).wait_recv()
-            own_d[...] += recv_d[p, off, pl.ds(0, nodes), :].astype(F32)
-            lines = lines + recv_d[p, off, pl.ds(nodes, EXTRA), :].astype(F32)
-        direct = own_d[...] + spread(lines)
+            take_xr(0, off)
+            if off <= 2:
+                take_xc(off - 1, 1)
+        reverse_products(0)
+        r_first(0)
+        for dist in range(2, max(3, chips - 1)):
+            take_xc(0, dist)
+            take_xc(1, dist)
+        visit(1)
+        for off in range(1, cols):
+            take_xr(1, off)
+        reverse_products(1)
+        r_first(1)
+        for dist in range(chips - 2, 0, -1):
+            r_relay(0, dist)
+            if dist == chips - 2:
+                take_xc(0, chips - 1)
+                take_xc(1, chips - 1)
+        direct_products(0)
+        for dist in range(chips - 2, 0, -1):
+            r_relay(1, dist)
+        visit(2)
+        direct_products(1)
         visit(3)
-        lines = jnp.zeros((EXTRA, width), F32)
-        for off in range(1, chips):
-            r_copy(off).wait_recv()
-            own_r[...] += recv_r[p, off, pl.ds(0, width), :].astype(F32)
-            lines = lines + recv_r[p, off, pl.ds(width, EXTRA), :].astype(F32)
-        reverse = jnp.transpose(own_r[...]) + spread(lines)
+        for h in range(2):
+            direct_total(h)
+            reverse_total(h)
         visit(4)
 
-        for off in range(1, cols):
-            xr_copy(off).wait_send()
-            d_copy(off).wait_send()
-        for off in range(cols):
-            xrs_copy(off, k).wait_send()
-        for off in range(1, chips):
-            r_copy(off).wait_send()
-
-        @pl.loop(0, chips)
-        def _(zz):
-            xcs_copy(k, zz).wait_send()
-
-        for dist in range(1, chips):
-
-            @pl.when(jnp.logical_and(z - dist + 1 >= 0, z + 1 < chips))
-            def _():
-                xcr_copy(dist, z - dist + 1).wait_send()
-
-            @pl.when(jnp.logical_and(z + dist - 1 < chips, z > 0))
-            def _():
-                xcl_copy(dist, z + dist - 1).wait_send()
-
-        return direct, reverse
+        for h in range(2):
+            for off in range(1, cols):
+                xr_copy(h, off).wait_send()
+                d_copy(h, off).wait_send()
+            for off in range(cols):
+                xrs_copy(h, off, k).wait_send()
+
+            @pl.loop(0, chips)
+            def _(zz):
+                xcs_copy(h, k, zz).wait_send()
+
+            for dist in range(1, chips):
+
+                @pl.when(z + dist < chips)
+                def _():
+                    r_copy(h, 0, z + dist).wait_send()
+
+                @pl.when(z - dist >= 0)
+                def _():
+                    r_copy(h, 1, z - dist).wait_send()
+
+                @pl.when(jnp.logical_and(z - dist + 1 >= 0, z + 1 < chips))
+                def _():
+                    xcr_copy(h, dist, z - dist + 1).wait_send()
+
+                @pl.when(jnp.logical_and(z + dist - 1 < chips, z > 0))
+                def _():
+                    xcl_copy(h, dist, z + dist - 1).wait_send()
+
+        return sums_d[...], sums_r[...]
 
     half = g_send.shape[0]
     depth = gz_send.shape[1]
@@ -546,6 +618,7 @@
     layers = weight_in.shape[0]
     slots, tile, unused = tile_values.shape
     chips = rows // 2
+    part_width = width // 2
     depth = -(-(3 * width + 8) // (rows * cols * 16)) * 16
     total = rows * cols * depth
     vmem = pl.BlockSpec(memory_space=pltpu.VMEM)
@@ -564,14 +637,16 @@
             pltpu.VMEM((2, cols * nodes, chips * nodes), BF16),
             pltpu.VMEM((cols * nodes, chips * nodes), BF16),
             pltpu.VMEM((slots, tile, tile), BF16),
-            pltpu.VMEM((2, 2, chips * nodes, width), BF16),
-            pltpu.VMEM((2, 2, width, cols * nodes), BF16),
-            pltpu.VMEM((cols, nodes + EXTRA, width), BF16),
-            pltpu.VMEM((2, cols, nodes + EXTRA, width), BF16),
-            pltpu.VMEM((chips, width + EXTRA, nodes), BF16),
-            pltpu.VMEM((2, chips, width + EXTRA, nodes), BF16),
+            pltpu.VMEM((2, 2, 2, chips * nodes, part_width), BF16),
+            pltpu.VMEM((2, 2, 2, part_width, cols * nodes), BF16),
+            pltpu.VMEM((2, cols, nodes + EXTRA, part_width), BF16),
+            pltpu.VMEM((2, 2, cols, nodes + EXTRA, part_width), BF16),
+            pltpu.VMEM((2, chips, part_width + EXTRA, nodes), BF16),
+            pltpu.VMEM((2, 2, 2, chips, part_width + EXTRA, nodes), BF16),
+            pltpu.VMEM((2, nodes, part_width), F32),
+            pltpu.VMEM((2, chips, part_width, nodes), F32),
             pltpu.VMEM((nodes, width), F32),
-            pltpu.VMEM((width, nodes), F32),
+            pltpu.VMEM((nodes, width), F32),
             pltpu.VMEM((nodes, width), F32),
             pltpu.VMEM((nodes, width), F32),
             pltpu.VMEM((layers + 1, nodes, width), BF16),
@@ -590,13 +665,13 @@
             pltpu.VMEM((layers, total, width), BF16),
             sems((rows,)),
             sems((2, 1)),
-            sems((2, 2, cols)),
-            sems((2, 2, cols)),
-            sems((2, 2, chips + 1)),
-            sems((2, 2, chips + 1)),
-            sems((2, 2, chips)),
-            sems((2, 2, cols)),
-            sems((2, 2, chips)),
+            sems((2, 2, 2 * cols)),
+            sems((2, 2, 2 * cols)),
+            sems((2, 2, 2 * (chips + 1))),
+            sems((2, 2, 2 * (chips + 1))),
+            sems((2, 2, 2 * chips)),
+            sems((2, 2, 2 * cols)),
+            sems((2, 2, 4 * chips)),
             sems((2, 2, 1)),
             sems((2, 2, cols)),
             sems((2, 2, chips)),

time: 164 us -> 151 us (0.921)
  Pallas kernels: 155 us -> 143 us
    pallas_call x1, Pallas kernels: 155 us -> 143 us  [per_device(): pl.pallas_call(functools.partial(kernel, rows, cols), out_shape=(jax.Shap...]
where the time goes in v3:
time: 151 us
  Pallas kernels  143 us (95%)
  local copies, waits for them, and re-layouts  6.81 us (5%)
    pallas_call x1, Pallas kernels, per_device(): pl.pallas_call(functools.partial(kernel, rows, cols), out_shape=(jax.Shap...  143 us
    unnamed x3, local copies, waits for them, and re-layouts  3.82 us

profile of v3, /device:TPU:0, one launch (start us, length us, event | category | flops | bytes accessed | tf_op | source)
XLA Modules:
  0.0 150.8 jit_solution(521207775084185174)
XLA Ops:
  1.3 142.7 %shard_map.154 = (bf16[256,256]{1,0:T(8,128)(2,1)}, f32[256,256]{1,0:T(8,128)}, bf16[2,1024,256]{2,1,0:T(8,128)(2,1)}) custom-call(bf16[256,256]{1,0:T(8,128)(2,1)} %feat.1, bf16[2,256,256]{2,1,0:T(8,128)(2,1)} %w_in.1, bf16[2,256,256]{2,1,0:T(8,128)(2,1)} %w_out.1, bf16[2,256,256]{2,1,0:T(8,128)(2,1)} %w_self.1, f32[2,256]{1,0:T(2,128)} %bias.1, ...), custom_call_target="tpu_custom_call" | custom-call | tf_op jit(solution)/shard_map/pallas_call | solution.py:627
  143.9 2.3 %fusion = (f32[2,256,256]{2,1,0:T(8,128)}, f32[2,256,256]{2,1,0:T(8,128)}, f32[2,256,256]{2,1,0:T(8,128)}) fusion(bf16[2,1024,256]{2,1,0:T(8,128)(2,1)} %get-tuple-element.11), kind=kLoop, calls=%fused_computation.1 | loop fusion | bytes 3145728 | tf_op jit(solution)/shard_map/slice | solution.py:704
  146.2 0.7 slice.19
  146.9 0.6 copy.19
  147.5 1.6 %copy.23 = bf16[256,256]{1,0:T(8,128)(2,1)} copy(bf16[256,256]{1,0:T(8,128)(2,1)} %get-tuple-element.21) | data formatting | bytes 262144
  149.1 1.7 %copy.24 = f32[256,256]{1,0:T(8,128)} copy(f32[256,256]{1,0:T(8,128)} %get-tuple-element.22) | data formatting | bytes 524288

commit v4 on v3

--- a/solution.py
+++ b/solution.py
@@ -190,7 +190,7 @@
     def window(zz):
         return pl.ds(pl.multiple_of(zz * nodes, nodes), nodes)
 
-    def exchange(stage, first, second_t, points=()):
+    def exchange(stage, first, second_t, points=(), centred=True):
         p = lax.rem(stage, 2)
 
         def visit(number):
@@ -225,12 +225,15 @@
 
         def d_copy(h, off):
             target = at_col(lax.rem(c + off, cols))
-            return remote(send_d.at[h, off], recv_d.at[p, h, off], d_sem, h * cols + off, target, p)
+            span = pl.ds(0, nodes + (EXTRA if centred else 0))
+            landing = recv_d.at[p, h, off, span]
+            return remote(send_d.at[h, off, span], landing, d_sem, h * cols + off, target, p)
 
         def r_copy(h, way, dest):
             target = at_chip(z + 1 if way == 0 else z - 1)
-            landing = recv_r.at[p, h, way, dest]
-            return remote(send_r.at[h, dest], landing, r_sem, (h * 2 + way) * chips + dest, target, p)
+            span = pl.ds(0, part_width + (EXTRA if centred else 0))
+            landing = recv_r.at[p, h, way, dest, span]
+            return remote(send_r.at[h, dest, span], landing, r_sem, (h * 2 + way) * chips + dest, target, p)
 
         for h in range(2):
             span = slice(h * part_width, (h + 1) * part_width)
@@ -307,6 +310,10 @@
                 )
 
         def r_send(h, way, dest, total):
+            if not centred:
+                send_r[h, dest, pl.ds(0, part_width), :] = total.astype(BF16)
+                r_copy(h, way, dest).start()
+                return
             means = []
             for part in range(sub):
                 mean = jnp.mean(total[:, part * tile : (part + 1) * tile], axis=1, keepdims=True)
@@ -320,8 +327,10 @@
 
         def r_take(h, way, dest):
             r_copy(h, way, dest).wait_recv()
+            rest = recv_r[p, h, way, dest, pl.ds(0, part_width), :].astype(F32)
+            if not centred:
+                return rest
             mean = recv_r[p, h, way, dest, pl.ds(part_width, EXTRA), pl.ds(0, part_width)]
-            rest = recv_r[p, h, way, dest, pl.ds(0, part_width), :].astype(F32)
             return rest + dot_tn(mean, spreader)
 
         def r_first(h):
@@ -357,6 +366,10 @@
 
                 @pl.when(off > 0)
                 def _():
+                    if not centred:
+                        send_d[h, off, pl.ds(0, nodes), :] = piece.astype(BF16)
+                        d_copy(h, off).start()
+                        return
                     heads = []
                     for part in range(sub):
                         span = slice(part * tile, (part + 1) * tile)
@@ -385,8 +398,11 @@
             for off in range(1, cols):
                 d_copy(h, off).wait_recv()
                 total = total + recv_d[p, h, off, pl.ds(0, nodes), :].astype(F32)
-                heads = heads + recv_d[p, h, off, pl.ds(nodes, EXTRA), :].astype(F32)
-            sums_d[:, pl.ds(h * part_width, part_width)] = total + spread(heads)
+                if centred:
+                    heads = heads + recv_d[p, h, off, pl.ds(nodes, EXTRA), :].astype(F32)
+            if centred:
+                total = total + spread(heads)
+            sums_d[:, pl.ds(h * part_width, part_width)] = total
 
         def reverse_total(h):
             @pl.when(z > 0)
@@ -413,21 +429,23 @@
             take_xr(1, off)
         reverse_products(1)
         r_first(1)
+        visit(2)
+        take_xc(0, chips - 1)
+        take_xc(1, chips - 1)
+        direct_products(0)
         for dist in range(chips - 2, 0, -1):
             r_relay(0, dist)
-            if dist == chips - 2:
-                take_xc(0, chips - 1)
-                take_xc(1, chips - 1)
-        direct_products(0)
+        visit(3)
+        direct_products(1)
         for dist in range(chips - 2, 0, -1):
             r_relay(1, dist)
-        visit(2)
-        direct_products(1)
-        visit(3)
-        for h in range(2):
-            direct_total(h)
-            reverse_total(h)
         visit(4)
+        direct_total(0)
+        reverse_total(0)
+        direct_total(1)
+        visit(5)
+        reverse_total(1)
+        visit(6)
 
         for h in range(2):
             for off in range(1, cols):
@@ -542,10 +560,14 @@
             for off in range(1, cols):
                 spread_col(off, c).start()
             spread_sibling(k, c).start()
+
+        def pass_on():
             for off in range(1, cols):
                 source = lax.rem(c + cols - off, cols)
                 spread_col(off, source).wait_recv()
                 spread_sibling(k, source).start()
+
+        def finish():
             for off in range(cols):
                 spread_sibling(other, lax.rem(c + off, cols)).wait_recv()
             to_sibling().wait_send()
@@ -558,7 +580,7 @@
             for off in range(cols):
                 spread_sibling(k, lax.rem(c + off, cols)).wait_send()
 
-        return start, over_cols, over_chips, back_chips, back_cols
+        return start, over_cols, over_chips, back_chips, back_cols, pass_on, finish
 
     g_full[...] = jnp.zeros(g_full.shape, F32)
 
@@ -587,9 +609,8 @@
         gz_ref[...] = grad_z
         back_in = jnp.transpose(s_out[...] * dot_nt(grad_z, w_in[layer])).astype(BF16)
         back_out = (s_in[...] * dot_nt(grad_z, w_out[layer])).astype(BF16)
-        direct, reverse = exchange(
-            layers + step, back_out, back_in, reduction(layer, lax.rem(layers + step, 2))
-        )
+        phases = reduction(layer, lax.rem(layers + step, 2))
+        direct, reverse = exchange(layers + step, back_out, back_in, phases, centred=False)
         up[...] = (
             s_out[...] * direct + s_in[...] * reverse + dot_nt(gz_ref[...], w_self[layer])
         )

time: 151 us -> 137 us (0.907)
  Pallas kernels: 143 us -> 129 us
    pallas_call x1, Pallas kernels: 143 us -> 129 us  [per_device(): pl.pallas_call(functools.partial(kernel, rows, cols), out_shape=(jax.Shap...]
where the time goes in v4:
time: 137 us
  Pallas kernels  129 us (94%)
  local copies, waits for them, and re-layouts  6.81 us (5%)
    pallas_call x1, Pallas kernels, per_device(): pl.pallas_call(functools.partial(kernel, rows, cols), out_shape=(jax.Shap...  129 us
    unnamed x3, local copies, waits for them, and re-layouts  3.82 us

profile of v4, /device:TPU:0, one launch (start us, length us, event | category | flops | bytes accessed | tf_op | source)
XLA Modules:
  0.0 137.1 jit_solution(7240533880498143757)
XLA Ops:
  1.3 129.0 %shard_map.154 = (bf16[256,256]{1,0:T(8,128)(2,1)}, f32[256,256]{1,0:T(8,128)}, bf16[2,1024,256]{2,1,0:T(8,128)(2,1)}) custom-call(bf16[256,256]{1,0:T(8,128)(2,1)} %feat.1, bf16[2,256,256]{2,1,0:T(8,128)(2,1)} %w_in.1, bf16[2,256,256]{2,1,0:T(8,128)(2,1)} %w_out.1, bf16[2,256,256]{2,1,0:T(8,128)(2,1)} %w_self.1, f32[2,256]{1,0:T(2,128)} %bias.1, ...), custom_call_target="tpu_custom_call" | custom-call | tf_op jit(solution)/shard_map/pallas_call | solution.py:648
  130.3 2.3 %fusion = (f32[2,256,256]{2,1,0:T(8,128)}, f32[2,256,256]{2,1,0:T(8,128)}, f32[2,256,256]{2,1,0:T(8,128)}) fusion(bf16[2,1024,256]{2,1,0:T(8,128)(2,1)} %get-tuple-element.11), kind=kLoop, calls=%fused_computation.1 | loop fusion | bytes 3145728 | tf_op jit(solution)/shard_map/slice | solution.py:725
  132.6 0.7 slice.19
  133.3 0.6 copy.19
  133.9 1.6 %copy.23 = bf16[256,256]{1,0:T(8,128)(2,1)} copy(bf16[256,256]{1,0:T(8,128)(2,1)} %get-tuple-element.21) | data formatting | bytes 262144
  135.5 1.7 %copy.24 = f32[256,256]{1,0:T(8,128)} copy(f32[256,256]{1,0:T(8,128)} %get-tuple-element.22) | data formatting | bytes 524288
